TPU v7x, 1024 devices: a whole 8x8x8 slice. The times are simulated.
1024 devices in a mesh: gx: 16 (over x, core), gy: 64 (over y, z).
Axes of the slice: x: 8, y: 8, z: 8, core: 2. Of those that a mesh axis runs over, the one named last changes fastest.
Arguments:
- multipoles: bfloat16 [165, 262144], P(None, ('gx', 'gy')), may hold values from -6 to 6
- operators: bfloat16 [64, 165, 165], replicated, may hold values from -0.125 to 0.125
- boundary: int32 [10, 131072], P(None, ('gx', 'gy')), may hold values from 0 to 1407, as said below
- pair_target: int32 [64, 131072], P(None, ('gx', 'gy')), may hold values from 0 to 255
- pair_source: int32 [64, 131072], P(None, ('gx', 'gy')), may hold values from 0 to 1535
- pair_count: int32 [64, 1024], P(None, ('gx', 'gy')), may hold values from 1 to 128, as said below
Outputs:
- local_expansions: float32 [165, 262144], P(None, ('gx', 'gy'))
Inputs may be any that keep to these rules, and one draw needn't show every extreme that they name: `boundary`: on every device and cut l, the list holds 128 distinct columns in increasing order, all below 256 + l * 128, and always includes column 256 + l * 128 - 1. `pair_count`: on every device, some class uses all 128 slots.
All inputs are finite; a program needn't handle non-finite values.
Results may differ from a plain program's by a relative error of at most 0.0003.
Values may be sent and summed in bfloat16 or wider, within the bound.
A program may use at most 64 MiB of HBM per device.

v0:
```python
import math

import jax
import jax.numpy as jnp
from jax import lax
from jax.sharding import PartitionSpec as P


def from_partner(block, axis, distance):
    count = lax.axis_size(axis)
    route = []
    for low in range(count):
        high = low | 1 << distance
        if high != low and high < count:
            route += [(low, high), (high, low)]
    return lax.ppermute(block, axis, route)


def translate(expansion, operators, sources, source_index, target_index, active):
    class_count = operators.shape[0]
    coefficients = operators.shape[1]
    block_size = math.gcd(class_count, 8)
    block_count = class_count // block_size

    def translate_block(partial_value, pieces):
        operator_block, source_rows, target_rows, active_rows = pieces
        gathered = jnp.take(sources, source_rows, axis=1)
        translated = jnp.einsum(
            "cij,jcs->ics", operator_block, gathered, preferred_element_type=jnp.float32
        )
        translated = jnp.where(active_rows[None], translated, 0.0)
        partial_value = partial_value.at[:, target_rows.reshape(-1)].add(
            translated.reshape(coefficients, -1)
        )
        return (partial_value, None)

    pieces = (
        operators.reshape(block_count, block_size, coefficients, coefficients),
        source_index.reshape(block_count, block_size, -1),
        target_index.reshape(block_count, block_size, -1),
        active.reshape(block_count, block_size, -1),
    )
    expansion, _ = lax.scan(translate_block, expansion, pieces)
    return expansion


def per_device(multipoles, operators, boundary, pair_target, pair_source, pair_count):
    coefficients, own_cells = multipoles.shape
    cut_count, sent_count = boundary.shape
    pool_width = own_cells + cut_count * sent_count
    active = lax.broadcasted_iota(jnp.int32, pair_target.shape, 1) < pair_count
    expansion = jnp.zeros((coefficients, pool_width), jnp.float32)
    cell_pool = multipoles
    for cut_level in range(cut_count):
        cut_bit = cut_count - 1 - cut_level
        exported = jnp.take(cell_pool, boundary[cut_level], axis=1)
        received = from_partner(exported, ("gx", "gy"), cut_bit)
        cell_pool = jnp.concatenate([cell_pool, received], axis=1)
    source_all = jnp.concatenate([pair_source, pair_target[::-1]], axis=1)
    target_all = jnp.concatenate([pair_target, pair_source[::-1]], axis=1)
    active_all = jnp.concatenate([active, active[::-1]], axis=1)
    expansion = translate(expansion, operators, cell_pool, source_all, target_all, active_all)
    for cut_level in reversed(range(cut_count)):
        first_column = own_cells + cut_level * sent_count
        outgoing = expansion[:, first_column : first_column + sent_count]
        returned = from_partner(outgoing, ("gx", "gy"), cut_count - 1 - cut_level)
        expansion = expansion[:, :first_column].at[:, boundary[cut_level]].add(returned)
    return expansion


def solution(mesh):
    in_specs = (
        P(None, ("gx", "gy")),
        P(),
        P(None, ("gx", "gy")),
        P(None, ("gx", "gy")),
        P(None, ("gx", "gy")),
        P(None, ("gx", "gy")),
    )
    out_specs = P(None, ("gx", "gy"))
    return jax.shard_map(
        per_device, mesh=mesh, in_specs=in_specs, out_specs=out_specs, check_vma=False
    )
```

profile of v0, /device:TPU:14, one launch (start us, length us, event | category | flops | bytes accessed | tf_op | source)
XLA Modules:
  0.0 453.6 jit_solution(4704032805487253518)
XLA Ops:
  24.6 9.5 %collective-permute-start.2 = (bf16[165,128]{0,1:T(8,128)(2,1)S(1)}, bf16[165,128]{0,1:T(8,128)(2,1)S(1)}, u32[]{:S(2)}, u32[]{:S(2)}) collective-permute-start(bf16[165,128]{0,1:T(8,128)(2,1)S(1)} %select_bitcast_fusion.7), channel_id=1, source_target_pairs={{0,128},{128,0},{1,129},{129,1},{2,130},{130,2},{3,131},{131,3},{4... | collective-permute-start | bytes 126728 | tf_op jit(solution)/shard_map/ppermute | solution.py:16
  45.4 7.5 %collective-permute-done.4 = bf16[165,128]{0,1:T(8,128)(2,1)S(1)} collective-permute-done((bf16[165,128]{0,1:T(8,128)(2,1)S(1)}, bf16[165,128]{0,1:T(8,128)(2,1)S(1)}, u32[]{:S(2)}, u32[]{:S(2)}) %collective-permute-start.4) | collective-permute-done | bytes 42272 | tf_op jit(solution)/shard_map/ppermute | solution.py:16
  71.0 10.7 %collective-permute-start.7 = (bf16[165,128]{0,1:T(8,128)(2,1)S(1)}, bf16[165,128]{0,1:T(8,128)(2,1)S(1)}, u32[]{:S(2)}, u32[]{:S(2)}) collective-permute-start(bf16[165,128]{0,1:T(8,128)(2,1)S(1)} %select_bitcast_fusion.2), channel_id=1, source_target_pairs={{0,4},{4,0},{1,5},{5,1},{2,6},{6,2},{3,7},{7,3},{8,12},{12,8},{9,1... | collective-permute-start | bytes 126728 | tf_op jit(solution)/shard_map/ppermute | solution.py:16
  102.3 8.0 %copy.35 = bf16[64,165,165]{2,1,0:T(8,128)(2,1)} copy(bf16[64,165,165]{2,0,1:T(8,128)(2,1)} %param.9) | data formatting | bytes 6969600 | tf_op args[1]
  110.4 230.6 %while.10 = (s32[]{:T(128)}, f32[165,1536]{0,1:T(8,128)S(1)}, s32[8,8,256]{2,1,0:T(8,128)}, pred[8,8,256]{2,1,0:T(8,128)(4,1)S(1)}, s32[8,8,256]{2,1,0:T(8,128)S...) while((s32[]{:T(128)}, f32[165,1536]{0,1:T(8,128)S(1)}, ...), condition=%wide.region_2.3_spmd, body=%wide.region_0.0_spmd.sunk | while | flops 112553984 | bytes 20506748 | solution.py:43
  111.3 7.5 %gather_fusion = bf16[2048,165]{1,0:T(8,128)(2,1)S(1)} fusion(bf16[165,1536]{0,1:T(8,128)(2,1)S(1)} %get-tuple-element.200, s32[2048]{0:T(1024)S(1)} %broadcast_clamp_fusion.2), kind=kCustom, calls=%fused_computation.clone.1 | custom fusion | bytes 1359872 | tf_op jit(solution)/shard_map/while/body/eval_jaxpr/jit(_take)/gather | solution.py:27
  126.7 12.6 %scatter_fusion = f32[165,1536]{0,1:T(8,128)S(1)} fusion(f32[165,1536]{0,1:T(8,128)S(1)} %get-tuple-element.187, s32[2048]{0:T(1024)S(1)} %bitcast.181, f32[2048,165]{1,0:T(8,128)} %copy.51), kind=kCustom, calls=%fused_computation.11.clone.1 | custom fusion | flops 337920 | bytes 4063232 | tf_op jit(solution)/shard_map/while/body/eval_jaxpr/scatter-add | solution.py:32
  140.1 7.5 %gather_fusion = bf16[2048,165]{1,0:T(8,128)(2,1)S(1)} fusion(bf16[165,1536]{0,1:T(8,128)(2,1)S(1)} %get-tuple-element.200, s32[2048]{0:T(1024)S(1)} %broadcast_clamp_fusion.2), kind=kCustom, calls=%fused_computation.clone.1 | custom fusion | bytes 1359872 | tf_op jit(solution)/shard_map/while/body/eval_jaxpr/jit(_take)/gather | solution.py:27
  155.5 12.6 %scatter_fusion = f32[165,1536]{0,1:T(8,128)S(1)} fusion(f32[165,1536]{0,1:T(8,128)S(1)} %get-tuple-element.187, s32[2048]{0:T(1024)S(1)} %bitcast.181, f32[2048,165]{1,0:T(8,128)} %copy.51), kind=kCustom, calls=%fused_computation.11.clone.1 | custom fusion | flops 337920 | bytes 4063232 | tf_op jit(solution)/shard_map/while/body/eval_jaxpr/scatter-add | solution.py:32
  168.9 7.5 %gather_fusion = bf16[2048,165]{1,0:T(8,128)(2,1)S(1)} fusion(bf16[165,1536]{0,1:T(8,128)(2,1)S(1)} %get-tuple-element.200, s32[2048]{0:T(1024)S(1)} %broadcast_clamp_fusion.2), kind=kCustom, calls=%fused_computation.clone.1 | custom fusion | bytes 1359872 | tf_op jit(solution)/shard_map/while/body/eval_jaxpr/jit(_take)/gather | solution.py:27
  184.3 12.6 %scatter_fusion = f32[165,1536]{0,1:T(8,128)S(1)} fusion(f32[165,1536]{0,1:T(8,128)S(1)} %get-tuple-element.187, s32[2048]{0:T(1024)S(1)} %bitcast.181, f32[2048,165]{1,0:T(8,128)} %copy.51), kind=kCustom, calls=%fused_computation.11.clone.1 | custom fusion | flops 337920 | bytes 4063232 | tf_op jit(solution)/shard_map/while/body/eval_jaxpr/scatter-add | solution.py:32
  197.7 7.5 %gather_fusion = bf16[2048,165]{1,0:T(8,128)(2,1)S(1)} fusion(bf16[165,1536]{0,1:T(8,128)(2,1)S(1)} %get-tuple-element.200, s32[2048]{0:T(1024)S(1)} %broadcast_clamp_fusion.2), kind=kCustom, calls=%fused_computation.clone.1 | custom fusion | bytes 1359872 | tf_op jit(solution)/shard_map/while/body/eval_jaxpr/jit(_take)/gather | solution.py:27
  213.2 12.6 %scatter_fusion = f32[165,1536]{0,1:T(8,128)S(1)} fusion(f32[165,1536]{0,1:T(8,128)S(1)} %get-tuple-element.187, s32[2048]{0:T(1024)S(1)} %bitcast.181, f32[2048,165]{1,0:T(8,128)} %copy.51), kind=kCustom, calls=%fused_computation.11.clone.1 | custom fusion | flops 337920 | bytes 4063232 | tf_op jit(solution)/shard_map/while/body/eval_jaxpr/scatter-add | solution.py:32
  226.6 7.5 %gather_fusion = bf16[2048,165]{1,0:T(8,128)(2,1)S(1)} fusion(bf16[165,1536]{0,1:T(8,128)(2,1)S(1)} %get-tuple-element.200, s32[2048]{0:T(1024)S(1)} %broadcast_clamp_fusion.2), kind=kCustom, calls=%fused_computation.clone.1 | custom fusion | bytes 1359872 | tf_op jit(solution)/shard_map/while/body/eval_jaxpr/jit(_take)/gather | solution.py:27
  242.0 12.6 %scatter_fusion = f32[165,1536]{0,1:T(8,128)S(1)} fusion(f32[165,1536]{0,1:T(8,128)S(1)} %get-tuple-element.187, s32[2048]{0:T(1024)S(1)} %bitcast.181, f32[2048,165]{1,0:T(8,128)} %copy.51), kind=kCustom, calls=%fused_computation.11.clone.1 | custom fusion | flops 337920 | bytes 4063232 | tf_op jit(solution)/shard_map/while/body/eval_jaxpr/scatter-add | solution.py:32
  255.4 7.5 %gather_fusion = bf16[2048,165]{1,0:T(8,128)(2,1)S(1)} fusion(bf16[165,1536]{0,1:T(8,128)(2,1)S(1)} %get-tuple-element.200, s32[2048]{0:T(1024)S(1)} %broadcast_clamp_fusion.2), kind=kCustom, calls=%fused_computation.clone.1 | custom fusion | bytes 1359872 | tf_op jit(solution)/shard_map/while/body/eval_jaxpr/jit(_take)/gather | solution.py:27
  270.8 12.6 %scatter_fusion = f32[165,1536]{0,1:T(8,128)S(1)} fusion(f32[165,1536]{0,1:T(8,128)S(1)} %get-tuple-element.187, s32[2048]{0:T(1024)S(1)} %bitcast.181, f32[2048,165]{1,0:T(8,128)} %copy.51), kind=kCustom, calls=%fused_computation.11.clone.1 | custom fusion | flops 337920 | bytes 4063232 | tf_op jit(solution)/shard_map/while/body/eval_jaxpr/scatter-add | solution.py:32
  284.2 7.5 %gather_fusion = bf16[2048,165]{1,0:T(8,128)(2,1)S(1)} fusion(bf16[165,1536]{0,1:T(8,128)(2,1)S(1)} %get-tuple-element.200, s32[2048]{0:T(1024)S(1)} %broadcast_clamp_fusion.2), kind=kCustom, calls=%fused_computation.clone.1 | custom fusion | bytes 1359872 | tf_op jit(solution)/shard_map/while/body/eval_jaxpr/jit(_take)/gather | solution.py:27
  299.7 12.6 %scatter_fusion = f32[165,1536]{0,1:T(8,128)S(1)} fusion(f32[165,1536]{0,1:T(8,128)S(1)} %get-tuple-element.187, s32[2048]{0:T(1024)S(1)} %bitcast.181, f32[2048,165]{1,0:T(8,128)} %copy.51), kind=kCustom, calls=%fused_computation.11.clone.1 | custom fusion | flops 337920 | bytes 4063232 | tf_op jit(solution)/shard_map/while/body/eval_jaxpr/scatter-add | solution.py:32
  313.1 7.5 %gather_fusion = bf16[2048,165]{1,0:T(8,128)(2,1)S(1)} fusion(bf16[165,1536]{0,1:T(8,128)(2,1)S(1)} %get-tuple-element.200, s32[2048]{0:T(1024)S(1)} %broadcast_clamp_fusion.2), kind=kCustom, calls=%fused_computation.clone.1 | custom fusion | bytes 1359872 | tf_op jit(solution)/shard_map/while/body/eval_jaxpr/jit(_take)/gather | solution.py:27
  328.5 12.6 %scatter_fusion = f32[165,1536]{0,1:T(8,128)S(1)} fusion(f32[165,1536]{0,1:T(8,128)S(1)} %get-tuple-element.187, s32[2048]{0:T(1024)S(1)} %bitcast.181, f32[2048,165]{1,0:T(8,128)} %copy.51), kind=kCustom, calls=%fused_computation.11.clone.1 | custom fusion | flops 337920 | bytes 4063232 | tf_op jit(solution)/shard_map/while/body/eval_jaxpr/scatter-add | solution.py:32
  362.9 7.9 %collective-permute-start.12 = (f32[165,128]{0,1:T(8,128)S(1)}, f32[165,128]{0,1:T(8,128)S(1)}, u32[]{:S(2)}, u32[]{:S(2)}) collective-permute-start(f32[165,128]{0,1:T(8,128)S(1)} %slice.155), channel_id=1, source_target_pairs={{0,4},{4,0},{1,5},{5,1},{2,6},{6,2},{3,7},{7,3},{8,12},{12,8},{9,1... | collective-permute-start | bytes 253448 | tf_op jit(solution)/shard_map/ppermute | solution.py:16
  390.8 7.6 %collective-permute-done.14 = f32[165,128]{0,1:T(8,128)S(1)} collective-permute-done((f32[165,128]{0,1:T(8,128)S(1)}, f32[165,128]{0,1:T(8,128)S(1)}, u32[]{:S(2)}, u32[]{:S(2)}) %collective-permute-start.14) | collective-permute-done | bytes 84512 | tf_op jit(solution)/shard_map/ppermute | solution.py:16
  443.1 8.3 %collective-permute-done.19 = f32[165,128]{0,1:T(8,128)S(1)} collective-permute-done((f32[165,128]{0,1:T(8,128)S(1)}, f32[165,128]{0,1:T(8,128)S(1)}, u32[]{:S(2)}, u32[]{:S(2)}) %collective-permute-start.19) | collective-permute-done | bytes 84512 | tf_op jit(solution)/shard_map/ppermute | solution.py:16
  (243 shorter events, 232.1 us)
Async XLA Ops:
  0.0 10.5 %copy-start = (s32[64,128]{1,0:T(8,128)S(1)}, s32[64,128]{1,0:T(8,128)}, u32[]{:S(2)}) copy-start(s32[64,128]{1,0:T(8,128)} %param.12) | copy-start | bytes 98308
  4.5 11.1 %collective-permute-start = (bf16[165,128]{0,1:T(8,128)(2,1)S(1)}, bf16[165,128]{0,1:T(8,128)(2,1)S(1)}, u32[]{:S(2)}, u32[]{:S(2)}) collective-permute-start(bf16[165,128]{0,1:T(8,128)(2,1)S(1)} %select_bitcast_fusion.9), channel_id=1, source_target_pairs={{0,512},{512,0},{1,513},{513,1},{2,514},{514,2},{3,515},{515,3},{4... | collective-permute-start | bytes 126728 | tf_op jit(solution)/shard_map/ppermute | solution.py:16
  16.6 7.1 %collective-permute-start.1 = (bf16[165,128]{0,1:T(8,128)(2,1)S(1)}, bf16[165,128]{0,1:T(8,128)(2,1)S(1)}, u32[]{:S(2)}, u32[]{:S(2)}) collective-permute-start(bf16[165,128]{0,1:T(8,128)(2,1)S(1)} %select_bitcast_fusion.8), channel_id=1, source_target_pairs={{0,256},{256,0},{1,257},{257,1},{2,258},{258,2},{3,259},{259,3},{4... | collective-permute-start | bytes 126728 | tf_op jit(solution)/shard_map/ppermute | solution.py:16
  24.6 11.8 %collective-permute-start.2 = (bf16[165,128]{0,1:T(8,128)(2,1)S(1)}, bf16[165,128]{0,1:T(8,128)(2,1)S(1)}, u32[]{:S(2)}, u32[]{:S(2)}) collective-permute-start(bf16[165,128]{0,1:T(8,128)(2,1)S(1)} %select_bitcast_fusion.7), channel_id=1, source_target_pairs={{0,128},{128,0},{1,129},{129,1},{2,130},{130,2},{3,131},{131,3},{4... | collective-permute-start | bytes 126728 | tf_op jit(solution)/shard_map/ppermute | solution.py:16
  37.4 3.1 collective-permute-start.3
  40.5 24.7 %copy-start.2 = (s32[128]{0:T(128)S(1)}, s32[128]{0:T(128)}, u32[]{:S(2)}) copy-start(s32[128]{0:T(128)} %get-tuple-element.130) | copy-start | bytes 1540
  42.0 39.7 %copy-start.3 = (s32[128]{0:T(128)S(1)}, s32[128]{0:T(128)}, u32[]{:S(2)}) copy-start(s32[128]{0:T(128)} %get-tuple-element.131) | copy-start | bytes 1540
  42.1 10.8 %collective-permute-start.4 = (bf16[165,128]{0,1:T(8,128)(2,1)S(1)}, bf16[165,128]{0,1:T(8,128)(2,1)S(1)}, u32[]{:S(2)}, u32[]{:S(2)}) collective-permute-start(bf16[165,128]{0,1:T(8,128)(2,1)S(1)} %select_bitcast_fusion.5), channel_id=1, source_target_pairs={{0,32},{32,0},{1,33},{33,1},{2,34},{34,2},{3,35},{35,3},{4,36},{36... | collective-permute-start | bytes 126728 | tf_op jit(solution)/shard_map/ppermute | solution.py:16
  54.5 38.3 %copy-start.4 = (s32[128]{0:T(128)S(1)}, s32[128]{0:T(128)}, u32[]{:S(2)}) copy-start(s32[128]{0:T(128)} %get-tuple-element.122) | copy-start | bytes 1540
  54.6 7.1 %collective-permute-start.5 = (bf16[165,128]{0,1:T(8,128)(2,1)S(1)}, bf16[165,128]{0,1:T(8,128)(2,1)S(1)}, u32[]{:S(2)}, u32[]{:S(2)}) collective-permute-start(bf16[165,128]{0,1:T(8,128)(2,1)S(1)} %select_bitcast_fusion.4), channel_id=1, source_target_pairs={{0,16},{16,0},{1,17},{17,1},{2,18},{18,2},{3,19},{19,3},{4,20},{20... | collective-permute-start | bytes 126728 | tf_op jit(solution)/shard_map/ppermute | solution.py:16
  63.3 6.2 %collective-permute-start.6 = (bf16[165,128]{0,1:T(8,128)(2,1)S(1)}, bf16[165,128]{0,1:T(8,128)(2,1)S(1)}, u32[]{:S(2)}, u32[]{:S(2)}) collective-permute-start(bf16[165,128]{0,1:T(8,128)(2,1)S(1)} %select_bitcast_fusion.3), channel_id=1, source_target_pairs={{0,8},{8,0},{1,9},{9,1},{2,10},{10,2},{3,11},{11,3},{4,12},{12,4},... | collective-permute-start | bytes 126728 | tf_op jit(solution)/shard_map/ppermute | solution.py:16
  71.0 13.0 %collective-permute-start.7 = (bf16[165,128]{0,1:T(8,128)(2,1)S(1)}, bf16[165,128]{0,1:T(8,128)(2,1)S(1)}, u32[]{:S(2)}, u32[]{:S(2)}) collective-permute-start(bf16[165,128]{0,1:T(8,128)(2,1)S(1)} %select_bitcast_fusion.2), channel_id=1, source_target_pairs={{0,4},{4,0},{1,5},{5,1},{2,6},{6,2},{3,7},{7,3},{8,12},{12,8},{9,1... | collective-permute-start | bytes 126728 | tf_op jit(solution)/shard_map/ppermute | solution.py:16
  86.7 8.3 %collective-permute-start.8 = (bf16[165,128]{0,1:T(8,128)(2,1)S(1)}, bf16[165,128]{0,1:T(8,128)(2,1)S(1)}, u32[]{:S(2)}, u32[]{:S(2)}) collective-permute-start(bf16[165,128]{0,1:T(8,128)(2,1)S(1)} %select_bitcast_fusion.1), channel_id=1, source_target_pairs={{0,2},{2,0},{1,3},{3,1},{4,6},{6,4},{5,7},{7,5},{8,10},{10,8},{9,1... | collective-permute-start | bytes 126728 | tf_op jit(solution)/shard_map/ppermute | solution.py:16
  97.7 12.6 %collective-permute-start.9 = (bf16[165,128]{0,1:T(8,128)(2,1)S(1)}, bf16[165,128]{0,1:T(8,128)(2,1)S(1)}, u32[]{:S(2)}, u32[]{:S(2)}) collective-permute-start(bf16[165,128]{0,1:T(8,128)(2,1)S(1)} %select_bitcast_fusion), channel_id=1, source_target_pairs={{0,1},{1,0},{2,3},{3,2},{4,5},{5,4},{6,7},{7,6},{8,9},{9,8},{10,11... | collective-permute-start | bytes 126728 | tf_op jit(solution)/shard_map/ppermute | solution.py:16
  341.1 6.9 %collective-permute-start.10 = (f32[165,128]{0,1:T(8,128)S(1)}, f32[165,128]{0,1:T(8,128)S(1)}, u32[]{:S(2)}, u32[]{:S(2)}) collective-permute-start(f32[165,128]{0,1:T(8,128)S(1)} %slice.111), channel_id=1, source_target_pairs={{0,1},{1,0},{2,3},{3,2},{4,5},{5,4},{6,7},{7,6},{8,9},{9,8},{10,11... | collective-permute-start | bytes 253448 | tf_op jit(solution)/shard_map/ppermute | solution.py:16
  352.5 8.6 %collective-permute-start.11 = (f32[165,128]{0,1:T(8,128)S(1)}, f32[165,128]{0,1:T(8,128)S(1)}, u32[]{:S(2)}, u32[]{:S(2)}) collective-permute-start(f32[165,128]{0,1:T(8,128)S(1)} %slice.153), channel_id=1, source_target_pairs={{0,2},{2,0},{1,3},{3,1},{4,6},{6,4},{5,7},{7,5},{8,10},{10,8},{9,1... | collective-permute-start | bytes 253448 | tf_op jit(solution)/shard_map/ppermute | solution.py:16
  362.9 11.8 %collective-permute-start.12 = (f32[165,128]{0,1:T(8,128)S(1)}, f32[165,128]{0,1:T(8,128)S(1)}, u32[]{:S(2)}, u32[]{:S(2)}) collective-permute-start(f32[165,128]{0,1:T(8,128)S(1)} %slice.155), channel_id=1, source_target_pairs={{0,4},{4,0},{1,5},{5,1},{2,6},{6,2},{3,7},{7,3},{8,12},{12,8},{9,1... | collective-permute-start | bytes 253448 | tf_op jit(solution)/shard_map/ppermute | solution.py:16
  376.4 8.3 %collective-permute-start.13 = (f32[165,128]{0,1:T(8,128)S(1)}, f32[165,128]{0,1:T(8,128)S(1)}, u32[]{:S(2)}, u32[]{:S(2)}) collective-permute-start(f32[165,128]{0,1:T(8,128)S(1)} %slice.157), channel_id=1, source_target_pairs={{0,8},{8,0},{1,9},{9,1},{2,10},{10,2},{3,11},{11,3},{4,12},{12,4},... | collective-permute-start | bytes 253448 | tf_op jit(solution)/shard_map/ppermute | solution.py:16
  386.4 12.0 %collective-permute-start.14 = (f32[165,128]{0,1:T(8,128)S(1)}, f32[165,128]{0,1:T(8,128)S(1)}, u32[]{:S(2)}, u32[]{:S(2)}) collective-permute-start(f32[165,128]{0,1:T(8,128)S(1)} %slice.159), channel_id=1, source_target_pairs={{0,16},{16,0},{1,17},{17,1},{2,18},{18,2},{3,19},{19,3},{4,20},{20... | collective-permute-start | bytes 253448 | tf_op jit(solution)/shard_map/ppermute | solution.py:16
  400.2 12.2 %collective-permute-start.15 = (f32[165,128]{0,1:T(8,128)S(1)}, f32[165,128]{0,1:T(8,128)S(1)}, u32[]{:S(2)}, u32[]{:S(2)}) collective-permute-start(f32[165,128]{0,1:T(8,128)S(1)} %slice.161), channel_id=1, source_target_pairs={{0,32},{32,0},{1,33},{33,1},{2,34},{34,2},{3,35},{35,3},{4,36},{36... | collective-permute-start | bytes 253448 | tf_op jit(solution)/shard_map/ppermute | solution.py:16
  414.0 3.2 collective-permute-start.16
  418.8 7.4 %collective-permute-start.17 = (f32[165,128]{0,1:T(8,128)S(1)}, f32[165,128]{0,1:T(8,128)S(1)}, u32[]{:S(2)}, u32[]{:S(2)}) collective-permute-start(f32[165,128]{0,1:T(8,128)S(1)} %slice.165), channel_id=1, source_target_pairs={{0,128},{128,0},{1,129},{129,1},{2,130},{130,2},{3,131},{131,3},{4... | collective-permute-start | bytes 253448 | tf_op jit(solution)/shard_map/ppermute | solution.py:16
  427.8 10.3 %collective-permute-start.18 = (f32[165,128]{0,1:T(8,128)S(1)}, f32[165,128]{0,1:T(8,128)S(1)}, u32[]{:S(2)}, u32[]{:S(2)}) collective-permute-start(f32[165,128]{0,1:T(8,128)S(1)} %slice.167), channel_id=1, source_target_pairs={{0,256},{256,0},{1,257},{257,1},{2,258},{258,2},{3,259},{259,3},{4... | collective-permute-start | bytes 253448 | tf_op jit(solution)/shard_map/ppermute | solution.py:16
  439.6 11.8 %collective-permute-start.19 = (f32[165,128]{0,1:T(8,128)S(1)}, f32[165,128]{0,1:T(8,128)S(1)}, u32[]{:S(2)}, u32[]{:S(2)}) collective-permute-start(f32[165,128]{0,1:T(8,128)S(1)} %slice.169), channel_id=1, source_target_pairs={{0,512},{512,0},{1,513},{513,1},{2,514},{514,2},{3,515},{515,3},{4... | collective-permute-start | bytes 253448 | tf_op jit(solution)/shard_map/ppermute | solution.py:16
  (2 other events, 20.8 us)
where the time goes:
time: 456 us; the launch traced here: 454 us
  local copies, waits for them, and re-layouts  147 us (32%)
  other arithmetic  123 us (27%)
  starting transfers between devices  86.9 us (19%)
  waiting for transfers between devices  81.5 us (18%)
  matrix products  13.1 us (3%)
    scatter-add x8, other arithmetic, translate_block(): partial_value.at[:, target_rows.reshape(-1)]  100 us
    ppermute x20, starting transfers between devices, from_partner(): return lax.ppermute(block, axis, route)  86.9 us
    ppermute x20, waiting for transfers between devices, from_partner(): return lax.ppermute(block, axis, route)  81.5 us
    gather x16, local copies, waits for them, and re-layouts, translate_block(): gathered = jnp.take(sources, source_rows, axis=1)  70.1 us
    reshape x8, local copies, waits for them, and re-layouts, translate_block(): translated.reshape(coefficients, -1)  22.2 us
    while x40, local copies, waits for them, and re-layouts  20 us
    scatter-add x10, other arithmetic, per_device(): expansion[:, :first_column].at[:, boundary[cut_level]].add(returned)  18.1 us
    unnamed x23, local copies, waits for them, and re-layouts  15.2 us
  transfers between devices with their start and end apart: 20, of which 19 were waited for; matrix products, arithmetic and copies ran while one was open for 3% of the time, Pallas kernels for 0%

commit v1 on v0

v1 whole, which is shorter than its diff:
```python
import functools

import jax
import jax.numpy as jnp
from jax import lax
from jax.experimental import pallas as pl
from jax.experimental.pallas import tpu as pltpu
from jax.sharding import PartitionSpec as P

MESH = pl.DeviceIdType.MESH
BLOCK = 128
NT = (((1,), (1,)), ((), ()))
NN = (((1,), (0,)), ((), ()))

FLIGHT_OUT = {0: 1.5, 1: 2.5, 2: 4.0, 4: 6.0}
FLIGHT_BACK = {0: 2.0, 1: 3.5, 2: 6.0, 4: 9.0}
COST = {"terms": 9.0, "scatter": 2.4, "gather": 3.5, "out": 0.6, "back": 1.0}


def plan(distance, tiles, gathers):
    cuts = len(distance)
    order = [("R", 0), ("S", (tiles - 1, 0)), ("S", (tiles - 1, 1)), ("send", cuts - 1)]
    now = COST["terms"] + 2 * COST["scatter"]
    out, back = 0, cuts - 1
    out_due = FLIGHT_OUT[distance[0]]
    back_due = now + FLIGHT_BACK[distance[back]]
    scatters = [(tile, half) for tile in range(tiles - 2, -1, -1) for half in range(2)]
    gathers = list(range(gathers))
    while out < cuts or back >= 0 or scatters or gathers:
        if out < cuts and out_due <= now:
            order.append(("F", out))
            now += COST["out"]
            out += 1
            if out < cuts:
                out_due = now + FLIGHT_OUT[distance[out]]
            continue
        needed = bool(scatters) and back > 0 and (back + 1) // 2 <= scatters[0][0]
        if back >= 0 and back_due <= now and not needed:
            order.append(("B", back))
            now += COST["back"]
            back -= 1
            if back >= 0:
                back_due = now + FLIGHT_BACK[distance[back]]
            continue
        if scatters:
            order.append(("S", scatters.pop(0)))
            now += COST["scatter"]
        elif out == cuts and gathers:
            order.append(("G", gathers.pop(0)))
            now += COST["gather"]
        else:
            now = min([out_due] * (out < cuts) + [back_due] * (back >= 0))
    return order


def selector(index_row, first, rows):
    row = lax.broadcasted_iota(jnp.int32, (rows, index_row.shape[1]), 0) + first
    return jnp.where(row == index_row, 1.0, 0.0).astype(jnp.bfloat16)


def dot(a, b, dims=NN):
    return lax.dot_general(a, b, dims, preferred_element_type=jnp.float32)


def kernel(axes, order, multipoles, operators_hbm, boundary, pair_target, pair_source, pair_count, out,
           operators, pool, export, partial, target, source, terms, tile_sum, sums, returned, own,
           load_sem, out_send, out_recv, back_send, back_recv):
    cuts = boundary.shape[0]
    classes = pair_target.shape[0]
    coefficients = multipoles.shape[0]
    pairs = classes // 2
    low = terms.shape[1] // 2
    blocks = cuts + 2

    load = pltpu.make_async_copy(operators_hbm, operators, load_sem)
    load.start()

    def partner(cut):
        bit = cuts - 1 - cut
        inner = axes[1][1].bit_length() - 1
        name, shift = (axes[1][0], bit) if bit < inner else (axes[0][0], bit - inner)
        me = lax.axis_index(name)
        step = 1 << shift
        other = me + step - 2 * step * ((me // step) % 2)
        here = {axes[0][0]: lax.axis_index(axes[0][0]), axes[1][0]: lax.axis_index(axes[1][0])}
        here[name] = other
        return (here[axes[0][0]], here[axes[1][0]])

    barrier = pltpu.get_barrier_semaphore()
    for cut in range(cuts):
        pl.semaphore_signal(barrier, inc=1, device_id=partner(cut), device_id_type=MESH)

    def outgoing(cut):
        return pltpu.make_async_remote_copy(
            src_ref=export.at[cut], dst_ref=pool.at[cut + 2], send_sem=out_send.at[cut],
            recv_sem=out_recv.at[cut], device_id=partner(cut), device_id_type=MESH)

    def incoming(cut):
        return pltpu.make_async_remote_copy(
            src_ref=sums.at[cut + 2], dst_ref=returned.at[cut], send_sem=back_send.at[cut],
            recv_sem=back_recv.at[cut], device_id=partner(cut), device_id_type=MESH)

    def chosen(cut, first, count):
        index = boundary[pl.ds(cut, 1), :]
        total = None
        for block in range(first, first + count):
            term = dot(pool[block], selector(index, block * BLOCK, BLOCK))
            total = term if total is None else total + term
        return total

    def prepare(cut):
        if cut < cuts:
            partial[...] = chosen(cut, 0, cut + 1)

    def send_out(cut):
        if cut < cuts:
            value = partial[...] + chosen(cut, cut + 1, 1)
            export[cut] = value.astype(jnp.bfloat16)
            outgoing(cut).start()
            prepare(cut + 1)

    def split(value):
        high = value.astype(jnp.bfloat16)
        return high, (value - high.astype(jnp.float32)).astype(jnp.bfloat16)

    def add_back(cut, first, count):
        index = boundary[pl.ds(cut, 1), :]
        high, rest = split(returned[cut])
        for block in range(first, first + count):
            chooser = selector(index, block * BLOCK, BLOCK)
            sums[block] += dot(high, chooser, NT) + dot(rest, chooser, NT)

    def index_pair(ref, pair):
        return jnp.concatenate([ref[pl.ds(2 * pair, 1), :], ref[pl.ds(2 * pair + 1, 1), :]], axis=1)

    def apply(pair, value, reverse):
        results = []
        for half in range(2):
            cls = 2 * pair + half
            matrix = operators[classes - 1 - cls] if reverse else operators[cls]
            results.append(dot(matrix, value[:, half * BLOCK : (half + 1) * BLOCK]))
        return split(jnp.concatenate(results, axis=1))

    def reverse_terms():
        mine = multipoles[...]

        def one(pair):
            columns = dot(mine, selector(index_pair(target, pair), 0, mine.shape[1])).astype(jnp.bfloat16)
            high, rest = apply(pair, columns, True)
            terms[pair, 0:coefficients, :] = high
            terms[pair, low : low + coefficients, :] = rest

        def body(step, carry):
            for part in range(4):
                one(4 * step + part)
            return carry

        lax.fori_loop(0, pairs // 4, body, 0)

    def scatter(tile, part):
        tile_sum[...] = jnp.zeros_like(tile_sum)

        def body(step, carry):
            total = None
            for half in range(2):
                pair = 2 * step + half
                term = dot(terms[pair], selector(index_pair(source, pair), tile * 2 * BLOCK, 2 * BLOCK), NT)
                total = term if total is None else total + term
            tile_sum[...] += total
            return carry

        lax.fori_loop(part * pairs // 4, (part + 1) * pairs // 4, body, 0)
        total = tile_sum[0:coefficients, :] + tile_sum[low : low + coefficients, :]
        sums[2 * tile] += total[:, :BLOCK]
        sums[2 * tile + 1] += total[:, BLOCK:]

    def gather(part, parts):
        def one(pair):
            index = index_pair(source, pair)
            total = None
            for tile in range(blocks // 2):
                columns = jnp.concatenate([pool[2 * tile], pool[2 * tile + 1]], axis=1)
                term = dot(columns, selector(index, tile * 2 * BLOCK, 2 * BLOCK))
                total = term if total is None else total + term
            high, rest = apply(pair, total.astype(jnp.bfloat16), False)
            chooser = selector(index_pair(target, pair), 0, 2 * BLOCK)
            return dot(high, chooser, NT) + dot(rest, chooser, NT)

        def body(step, carry):
            own[...] += one(2 * step) + one(2 * step + 1)
            return carry

        size = pairs // parts // 2
        lax.fori_loop(part * size, (part + 1) * size, body, 0)

    pool[0] = multipoles[:, :BLOCK]
    pool[1] = multipoles[:, BLOCK:]
    slot = lax.broadcasted_iota(jnp.int32, pair_target.shape, 1)
    active = slot < pair_count[...]
    target[...] = jnp.where(active, pair_target[...], -1)
    source[...] = jnp.where(active, pair_source[...], -1)
    prepare(0)
    pl.semaphore_wait(barrier, cuts)
    send_out(0)
    sums[...] = jnp.zeros_like(sums)
    own[...] = jnp.zeros_like(own)

    gathers = sum(kind == "G" for kind, _ in order)
    for kind, number in order:
        if kind == "R":
            load.wait()
            reverse_terms()
        elif kind == "S":
            scatter(*number)
        elif kind == "G":
            gather(number, gathers)
        elif kind == "send":
            incoming(number).start()
        elif kind == "F":
            outgoing(number).wait_recv()
            send_out(number + 1)
        else:
            incoming(number).wait_recv()
            if number > 0:
                add_back(number, number + 1, 1)
                incoming(number - 1).start()
                add_back(number, 0, number + 1)
            else:
                add_back(number, 0, 2)
    out[:, :BLOCK] = sums[0] + own[:, :BLOCK]
    out[:, BLOCK:] = sums[1] + own[:, BLOCK:]
    for cut in range(cuts):
        outgoing(cut).wait_send()
        incoming(cut).wait_send()


def per_device(axes, order, multipoles, operators, boundary, pair_target, pair_source, pair_count):
    coefficients, cells = multipoles.shape
    cuts = boundary.shape[0]
    classes, slots = pair_target.shape
    vmem = pl.BlockSpec(memory_space=pltpu.VMEM)
    half_rows = -(-coefficients // 16) * 16
    return pl.pallas_call(
        functools.partial(kernel, axes, order),
        out_shape=jax.ShapeDtypeStruct((coefficients, cells), jnp.float32),
        in_specs=[vmem, pl.BlockSpec(memory_space=pl.ANY), vmem, vmem, vmem, vmem],
        out_specs=vmem,
        scratch_shapes=[
            pltpu.VMEM(operators.shape, jnp.bfloat16),
            pltpu.VMEM((cuts + 2, coefficients, BLOCK), jnp.bfloat16),
            pltpu.VMEM((cuts, coefficients, BLOCK), jnp.bfloat16),
            pltpu.VMEM((coefficients, BLOCK), jnp.float32),
            pltpu.VMEM((classes, slots), jnp.int32),
            pltpu.VMEM((classes, slots), jnp.int32),
            pltpu.VMEM((classes // 2, 2 * half_rows, 2 * slots), jnp.bfloat16),
            pltpu.VMEM((2 * half_rows, 2 * BLOCK), jnp.float32),
            pltpu.VMEM((cuts + 2, coefficients, BLOCK), jnp.float32),
            pltpu.VMEM((cuts, coefficients, BLOCK), jnp.float32),
            pltpu.VMEM((coefficients, cells), jnp.float32),
            pltpu.SemaphoreType.DMA,
            pltpu.SemaphoreType.DMA((cuts,)),
            pltpu.SemaphoreType.DMA((cuts,)),
            pltpu.SemaphoreType.DMA((cuts,)),
            pltpu.SemaphoreType.DMA((cuts,)),
        ],
        compiler_params=pltpu.CompilerParams(
            collective_id=0, has_side_effects=True, vmem_limit_bytes=60 << 20),
    )(multipoles, operators, boundary, pair_target, pair_source, pair_count)


def solution(mesh):
    axes = tuple((name, mesh.shape[name]) for name in ("gx", "gy"))
    cuts = (axes[0][1] * axes[1][1]).bit_length() - 1
    distance = [4, 2, 1, 0, 4, 2, 1, 4, 2, 1] if cuts == 10 else [1] * cuts
    order = plan(distance, (cuts + 2) // 2, 8)
    spec = P(None, ("gx", "gy"))
    return jax.shard_map(
        functools.partial(per_device, axes, order), mesh=mesh,
        in_specs=(spec, P(), spec, spec, spec, spec), out_specs=spec, check_vma=False)
```

time: 456 us -> 114 us (0.25)
  local copies, waits for them, and re-layouts: 147 us -> 10.9 us
  other arithmetic: 123 us -> 0 us
  Pallas kernels: 0 us -> 103 us
  starting transfers between devices: 86.9 us -> 0 us
  waiting for transfers between devices: 81.5 us -> 0 us
  matrix products: 13.1 us -> 0 us
    scatter-add x18 -> x0, other arithmetic: 119 us -> none  [the longest x8 100 us: translate_block(): partial_value.at[:, target_rows.reshape(-1)]]
    pallas_call x0 -> x1, Pallas kernels: none -> 103 us  [per_device(): pl.pallas_call(functools.partial(kernel, axes, order), out_shape=jax.Shap...]
    ppermute x20 -> x0, starting transfers between devices: 86.9 us -> none  [from_partner(): return lax.ppermute(block, axis, route)]
    ppermute x20 -> x0, waiting for transfers between devices: 81.5 us -> none  [from_partner(): return lax.ppermute(block, axis, route)]
    gather x26 -> x0, local copies, waits for them, and re-layouts: 80.7 us -> none  [the longest x16 70.1 us: translate_block(): gathered = jnp.take(sources, source_rows, axis=1)]
    reshape x8 -> x0, local copies, waits for them, and re-layouts: 22.2 us -> none  [translate_block(): translated.reshape(coefficients, -1)]
    while x40 -> x0, local copies, waits for them, and re-layouts: 20 us -> none
    dot_general x8 -> x0, matrix products: 13.1 us -> none  [translate_block(): jnp.einsum('cij,jcs->ics', operator_block, gathered, preferred_element_ty...]
  transfers between devices with their start and end apart: 20 -> 0, of which waited for: 19 -> 0; matrix products, arithmetic and copies ran while one was open for 3% -> 0% of each run, Pallas kernels for 0% -> 0%
where the time goes in v1:
time: 114 us; the launch traced here: 113 us
  Pallas kernels  103 us (90%)
  local copies, waits for them, and re-layouts  10.9 us (10%)
    pallas_call x1, Pallas kernels, per_device(): pl.pallas_call(functools.partial(kernel, axes, order), out_shape=jax.Shap...  103 us
    unnamed x3, local copies, waits for them, and re-layouts  10.9 us

profile of v1, /device:TPU:14, one launch (start us, length us, event | category | flops | bytes accessed | tf_op | source)
XLA Modules:
  0.0 113.5 jit_solution(13107891321023363313)
XLA Ops:
  0.0 1.4 %copy.8.pair_count = s32[64,1]{1,0:T(8,128)} copy(s32[64,1]{0,1:T(1,128)} %param.11) | data formatting | bytes 512 | tf_op args[5]
  1.4 8.0 %copy.7.operators_hbm = bf16[64,165,165]{2,1,0:T(8,128)(2,1)} copy(bf16[64,165,165]{2,0,1:T(8,128)(2,1)} %param.7) | data formatting | bytes 6969600 | tf_op args[1]
  9.3 102.5 %shard_map.64 = f32[165,256]{1,0:T(8,128)} custom-call(bf16[165,256]{1,0:T(8,128)(2,1)} %multipoles.1, bf16[64,165,165]{2,1,0:T(8,128)(2,1)} %copy.7.operators_hbm, s32[10,128]{1,0:T(8,128)} %boundary.1, s32[64,128]{1,0:T(8,128)} %pair_target.1, s32[64,128]{1,0:T(8,128)} %pair_source.1, s32[64,1]{1,0:T(8,128)} %copy.8.pair_count), custom_call_target="tpu_custom_call" | custom-call | tf_op jit(solution)/shard_map/pallas_call | solution.py:243
  111.9 1.6 %copy.10 = f32[165,256]{1,0:T(8,128)} copy(f32[165,256]{1,0:T(8,128)} %shard_map.64) | data formatting | bytes 337920

commit v2 on v1

--- a/solution.py
+++ b/solution.py
@@ -14,7 +14,7 @@
 
 FLIGHT_OUT = {0: 1.5, 1: 2.5, 2: 4.0, 4: 6.0}
 FLIGHT_BACK = {0: 2.0, 1: 3.5, 2: 6.0, 4: 9.0}
-COST = {"terms": 9.0, "scatter": 2.4, "gather": 3.5, "out": 0.6, "back": 1.0}
+COST = {"terms": 9.5, "scatter": 2.4, "gather": 3.5, "out": 0.6, "back": 0.8}
 
 
 def plan(distance, tiles, gathers):
@@ -63,7 +63,7 @@
 
 
 def kernel(axes, order, multipoles, operators_hbm, boundary, pair_target, pair_source, pair_count, out,
-           operators, pool, export, partial, target, source, terms, tile_sum, sums, returned, own,
+           stage, left, right, operators, pool, export, partial, target, source, terms, tile_sum, sums, returned, own,
            load_sem, out_send, out_recv, back_send, back_recv):
     cuts = boundary.shape[0]
     classes = pair_target.shape[0]
@@ -71,9 +71,13 @@
     pairs = classes // 2
     low = terms.shape[1] // 2
     blocks = cuts + 2
-
-    load = pltpu.make_async_copy(operators_hbm, operators, load_sem)
-    load.start()
+    rows = sums.shape[1]
+    groups, _, group, _ = stage.shape
+
+    loads = [pltpu.make_async_copy(operators_hbm.at[:, pl.ds(g * group, group), :], stage.at[g], load_sem.at[g])
+             for g in range(groups)]
+    for load in reversed(loads):
+        load.start()
 
     def partner(cut):
         bit = cuts - 1 - cut
@@ -97,14 +101,16 @@
 
     def incoming(cut):
         return pltpu.make_async_remote_copy(
-            src_ref=sums.at[cut + 2], dst_ref=returned.at[cut], send_sem=back_send.at[cut],
+            src_ref=sums.at[cut + 2], dst_ref=returned.at[cut, pl.ds(0, rows), :], send_sem=back_send.at[cut],
             recv_sem=back_recv.at[cut], device_id=partner(cut), device_id_type=MESH)
 
     def chosen(cut, first, count):
         index = boundary[pl.ds(cut, 1), :]
         total = None
-        for block in range(first, first + count):
-            term = dot(pool[block], selector(index, block * BLOCK, BLOCK))
+        for block in range(first, first + count, 2):
+            size = min(2, first + count - block)
+            columns = pool[block] if size == 1 else jnp.concatenate([pool[block], pool[block + 1]], axis=1)
+            term = dot(columns, selector(index, block * BLOCK, size * BLOCK))
             total = term if total is None else total + term
         return total
 
@@ -121,14 +127,19 @@
 
     def split(value):
         high = value.astype(jnp.bfloat16)
-        return high, (value - high.astype(jnp.float32)).astype(jnp.bfloat16)
+        return jnp.concatenate([high, (value - high.astype(jnp.float32)).astype(jnp.bfloat16)], axis=0)
+
+    def joined(value):
+        return value[:rows] + value[low : low + rows]
 
     def add_back(cut, first, count):
         index = boundary[pl.ds(cut, 1), :]
-        high, rest = split(returned[cut])
-        for block in range(first, first + count):
-            chooser = selector(index, block * BLOCK, BLOCK)
-            sums[block] += dot(high, chooser, NT) + dot(rest, chooser, NT)
+        parts = split(returned[cut])
+        for block in range(first, first + count, 2):
+            size = min(2, first + count - block)
+            total = joined(dot(parts, selector(index, block * BLOCK, size * BLOCK), NT))
+            for part in range(size):
+                sums[block + part] += total[:, part * BLOCK : (part + 1) * BLOCK]
 
     def index_pair(ref, pair):
         return jnp.concatenate([ref[pl.ds(2 * pair, 1), :], ref[pl.ds(2 * pair + 1, 1), :]], axis=1)
@@ -146,16 +157,23 @@
 
         def one(pair):
             columns = dot(mine, selector(index_pair(target, pair), 0, mine.shape[1])).astype(jnp.bfloat16)
-            high, rest = apply(pair, columns, True)
-            terms[pair, 0:coefficients, :] = high
-            terms[pair, low : low + coefficients, :] = rest
+            terms[pair] = apply(pair, columns, True)
 
         def body(step, carry):
-            for part in range(4):
-                one(4 * step + part)
+            here = groups - 1 - step
+            plain = stage[here].astype(jnp.float32).reshape(coefficients * group, coefficients)
+            left[...] = plain[:, :BLOCK]
+            right[:, : coefficients - BLOCK] = plain[:, BLOCK:]
+            for cls in range(group):
+                every = pl.ds(cls, coefficients, stride=group)
+                operators[here * group + cls, 0:coefficients, :BLOCK] = left[every, :].astype(jnp.bfloat16)
+                matrix = right[every, :].astype(jnp.bfloat16)
+                operators[here * group + cls, 0:coefficients, BLOCK:] = matrix[:, : coefficients - BLOCK]
+            for part in range(group // 2):
+                one(step * (group // 2) + part)
             return carry
 
-        lax.fori_loop(0, pairs // 4, body, 0)
+        lax.fori_loop(0, groups, body, 0)
 
     def scatter(tile, part):
         tile_sum[...] = jnp.zeros_like(tile_sum)
@@ -170,7 +188,7 @@
             return carry
 
         lax.fori_loop(part * pairs // 4, (part + 1) * pairs // 4, body, 0)
-        total = tile_sum[0:coefficients, :] + tile_sum[low : low + coefficients, :]
+        total = joined(tile_sum[...])
         sums[2 * tile] += total[:, :BLOCK]
         sums[2 * tile + 1] += total[:, BLOCK:]
 
@@ -182,9 +200,8 @@
                 columns = jnp.concatenate([pool[2 * tile], pool[2 * tile + 1]], axis=1)
                 term = dot(columns, selector(index, tile * 2 * BLOCK, 2 * BLOCK))
                 total = term if total is None else total + term
-            high, rest = apply(pair, total.astype(jnp.bfloat16), False)
             chooser = selector(index_pair(target, pair), 0, 2 * BLOCK)
-            return dot(high, chooser, NT) + dot(rest, chooser, NT)
+            return dot(apply(pair, total.astype(jnp.bfloat16), False), chooser, NT)
 
         def body(step, carry):
             own[...] += one(2 * step) + one(2 * step + 1)
@@ -196,7 +213,9 @@
     pool[0] = multipoles[:, :BLOCK]
     pool[1] = multipoles[:, BLOCK:]
     slot = lax.broadcasted_iota(jnp.int32, pair_target.shape, 1)
-    active = slot < pair_count[...]
+    same = lax.broadcasted_iota(jnp.int32, (classes, classes), 0) == lax.broadcasted_iota(jnp.int32, (classes, classes), 1)
+    counts = jnp.sum(jnp.where(same, pair_count[...], 0), axis=1, keepdims=True)
+    active = slot < counts
     target[...] = jnp.where(active, pair_target[...], -1)
     source[...] = jnp.where(active, pair_source[...], -1)
     prepare(0)
@@ -208,7 +227,8 @@
     gathers = sum(kind == "G" for kind, _ in order)
     for kind, number in order:
         if kind == "R":
-            load.wait()
+            for load in loads:
+                load.wait()
             reverse_terms()
         elif kind == "S":
             scatter(*number)
@@ -227,8 +247,10 @@
                 add_back(number, 0, number + 1)
             else:
                 add_back(number, 0, 2)
-    out[:, :BLOCK] = sums[0] + own[:, :BLOCK]
-    out[:, BLOCK:] = sums[1] + own[:, BLOCK:]
+    for half in range(2):
+        lanes = pl.ds(half * BLOCK, BLOCK)
+        mine = own[0:coefficients, lanes] + own[low : low + coefficients, lanes]
+        out[:, lanes] = sums[half, 0:coefficients, :] + mine
     for cut in range(cuts):
         outgoing(cut).wait_send()
         incoming(cut).wait_send()
@@ -240,13 +262,17 @@
     classes, slots = pair_target.shape
     vmem = pl.BlockSpec(memory_space=pltpu.VMEM)
     half_rows = -(-coefficients // 16) * 16
+    rows = -(-coefficients // 8) * 8
     return pl.pallas_call(
         functools.partial(kernel, axes, order),
         out_shape=jax.ShapeDtypeStruct((coefficients, cells), jnp.float32),
         in_specs=[vmem, pl.BlockSpec(memory_space=pl.ANY), vmem, vmem, vmem, vmem],
         out_specs=vmem,
         scratch_shapes=[
-            pltpu.VMEM(operators.shape, jnp.bfloat16),
+            pltpu.VMEM((classes // 8, coefficients, 8, coefficients), jnp.bfloat16),
+            pltpu.VMEM((coefficients * 8, BLOCK), jnp.float32),
+            pltpu.VMEM((coefficients * 8, BLOCK), jnp.float32),
+            pltpu.VMEM((classes, half_rows, coefficients), jnp.bfloat16),
             pltpu.VMEM((cuts + 2, coefficients, BLOCK), jnp.bfloat16),
             pltpu.VMEM((cuts, coefficients, BLOCK), jnp.bfloat16),
             pltpu.VMEM((coefficients, BLOCK), jnp.float32),
@@ -254,10 +280,10 @@
             pltpu.VMEM((classes, slots), jnp.int32),
             pltpu.VMEM((classes // 2, 2 * half_rows, 2 * slots), jnp.bfloat16),
             pltpu.VMEM((2 * half_rows, 2 * BLOCK), jnp.float32),
-            pltpu.VMEM((cuts + 2, coefficients, BLOCK), jnp.float32),
-            pltpu.VMEM((cuts, coefficients, BLOCK), jnp.float32),
-            pltpu.VMEM((coefficients, cells), jnp.float32),
-            pltpu.SemaphoreType.DMA,
+            pltpu.VMEM((cuts + 2, rows, BLOCK), jnp.float32),
+            pltpu.VMEM((cuts, half_rows, BLOCK), jnp.float32),
+            pltpu.VMEM((2 * half_rows, cells), jnp.float32),
+            pltpu.SemaphoreType.DMA((classes // 8,)),
             pltpu.SemaphoreType.DMA((cuts,)),
             pltpu.SemaphoreType.DMA((cuts,)),
             pltpu.SemaphoreType.DMA((cuts,)),
@@ -265,7 +291,7 @@
         ],
         compiler_params=pltpu.CompilerParams(
             collective_id=0, has_side_effects=True, vmem_limit_bytes=60 << 20),
-    )(multipoles, operators, boundary, pair_target, pair_source, pair_count)
+    )(multipoles, jnp.transpose(operators, (1, 0, 2)), boundary, pair_target, pair_source, pair_count.reshape(1, classes))
 
 
 def solution(mesh):

time: 114 us -> 105 us (0.921)
  local copies, waits for them, and re-layouts: 10.9 us -> 1.6 us
    unnamed x3 -> x1, local copies, waits for them, and re-layouts: 10.9 us -> 1.6 us
where the time goes in v2:
time: 105 us
  Pallas kernels  103 us (98%)
  local copies, waits for them, and re-layouts  1.6 us (2%)
    pallas_call x1, Pallas kernels, per_device(): pl.pallas_call(functools.partial(kernel, axes, order), out_shape=jax.Shap...  103 us

profile of v2, /device:TPU:14, one launch (start us, length us, event | category | flops | bytes accessed | tf_op | source)
XLA Modules:
  0.0 105.0 jit_solution(1132181449802762597)
XLA Ops:
  0.0 103.4 %shard_map.64 = f32[165,256]{1,0:T(8,128)} custom-call(bf16[165,256]{1,0:T(8,128)(2,1)} %multipoles.1, bf16[165,64,165]{2,1,0:T(8,128)(2,1)} %bitcast.2, s32[10,128]{1,0:T(8,128)} %boundary.1, s32[64,128]{1,0:T(8,128)} %pair_target.1, s32[64,128]{1,0:T(8,128)} %pair_source.1, s32[1,64]{1,0:T(1,128)} %bitcast.3), custom_call_target="tpu_custom_call" | custom-call | tf_op jit(solution)/shard_map/pallas_call | solution.py:266
  103.4 1.6 %copy.8 = f32[165,256]{1,0:T(8,128)} copy(f32[165,256]{1,0:T(8,128)} %shard_map.64) | data formatting | bytes 337920
